TPU v7x, 32 devices: a whole 2x2x4 slice. The times are simulated.
32 devices in a mesh: gx: 4 (over z), gz: 4 (over y, core), sa: 2 (over x).
Axes of the slice: x: 2, y: 2, z: 4, core: 2. Of those that a mesh axis runs over, the one named last changes fastest.
Arguments:
- forcing: float32 [3, 8, 128, 32, 256], P(None, 'sa', 'gx', 'gz'), may hold values from -60 to 60
- velocity: float32 [256], replicated, may hold values from 0.3 to 1.2
- wall_solve: float32 [256, 256], replicated, may hold values from -1 to 1.7
Outputs:
- basis: float32 [3, 8, 128, 32, 256], P(None, 'sa', 'gx', 'gz')
- factor: float32 [8, 8], replicated
All inputs are finite; a program needn't handle non-finite values.
Results may differ from a plain program's by a relative error of at most 0.00015.
Values sent between devices are 32-bit elements; how exact they have to be, the bound alone decides.
No kernel may reach another device: no remote copies, remote signals or barrier semaphores. Data moves between devices by JAX's collectives and lax.ppermute only.
A program may use at most 64 MiB of HBM per device.

v0:
```python
import jax
import jax.numpy as jnp
from jax import lax
from jax.sharding import PartitionSpec as P

step_length = 0.4
viscosity = 0.2


def extended(cells, sides, width):
    for axis, dim in sides:
        count = lax.axis_size(axis)
        head = lax.slice_in_dim(cells, 0, width, axis=dim)
        tail = lax.slice_in_dim(cells, cells.shape[dim] - width, cells.shape[dim], axis=dim)
        cells = jnp.concatenate(
            [
                lax.ppermute(tail, axis, [(i, (i + 1) % count) for i in range(count)]),
                cells,
                lax.ppermute(head, axis, [((i + 1) % count, i) for i in range(count)]),
            ],
            axis=dim,
        )
    return cells


def shear_of(velocity):
    inner = (velocity[2:] - velocity[:-2]) * 0.5
    return jnp.concatenate([velocity[1:2] - velocity[0:1], inner, velocity[-1:] - velocity[-2:-1]])


def upper_factor(gram):
    order_size = gram.shape[0]
    column_ids = jnp.arange(order_size)
    row_list = []
    for pivot_index in range(order_size):
        current_row = gram[pivot_index]
        for other_index in range(pivot_index):
            current_row = current_row - row_list[other_index][pivot_index] * row_list[other_index]
        current_row = jnp.where(
            column_ids >= pivot_index, current_row, jnp.zeros_like(current_row)
        ) / jnp.sqrt(current_row[pivot_index])
        row_list.append(current_row)
    return jnp.stack(row_list)


def upper_inverse(factor):
    order_size = factor.shape[0]
    identity_rows = jnp.eye(order_size, dtype=factor.dtype)
    row_list = [None] * order_size
    for pivot_index in range(order_size - 1, -1, -1):
        current_row = identity_rows[pivot_index]
        for other_index in range(pivot_index + 1, order_size):
            current_row = current_row - factor[pivot_index, other_index] * row_list[other_index]
        row_list[pivot_index] = current_row / factor[pivot_index, pivot_index]
    return jnp.stack(row_list)


def stencil(padded, velocity, shear_rate, adjoint):
    center = padded[:, :, 1:-1, 1:-1]
    east_side = padded[:, :, 2:, 1:-1]
    west_side = padded[:, :, :-2, 1:-1]
    north_side = padded[:, :, 1:-1, 2:]
    south_side = padded[:, :, 1:-1, :-2]
    direction = 1.0 if adjoint else -1.0
    change = direction * velocity * (east_side - west_side) * 0.5 + viscosity * (
        east_side + west_side + north_side + south_side - 4.0 * center
    )
    if adjoint:
        change = change.at[1].add(-shear_rate * center[0])
    else:
        change = change.at[0].add(-shear_rate * center[1])
    return (center, change)


def wall_apply(field, wall_solve):
    return jnp.matmul(field, wall_solve, precision=lax.Precision.HIGHEST)


def wall_adjoint(field, wall_solve):
    return jnp.matmul(field, wall_solve.T, precision=lax.Precision.HIGHEST)


def near_faces(field):
    return extended(field, (("gx", 2), ("gz", 3)), 1)


def shards(forcing, velocity, wall_solve):
    shear_rate = shear_of(velocity)
    columns = forcing.shape[1]
    entries = (
        3
        * forcing.shape[2]
        * lax.axis_size("gx")
        * forcing.shape[3]
        * lax.axis_size("gz")
        * forcing.shape[4]
    )
    current = forcing
    for repeat in range(2):
        center, change = stencil(near_faces(current), velocity, shear_rate, False)
        current = wall_apply(center + step_length * (change + forcing), wall_solve)
    partial_value = jnp.sum(current * current, axis=(0, 2, 3, 4))
    response = current
    current = response
    for repeat in range(2):
        solved = wall_adjoint(current, wall_solve)
        center, change = stencil(near_faces(solved), velocity, shear_rate, True)
        current = center + step_length * change + step_length * response
    gathered = lax.all_gather(current, "sa", axis=1, tiled=True)
    half_rows = gathered.shape[4] // lax.axis_size("sa")
    row_block = lax.dynamic_slice_in_dim(gathered, lax.axis_index("sa") * half_rows, half_rows, 4)
    gram_local = jnp.einsum(
        "cixzy,cjxzy->ij", row_block, row_block, precision=lax.Precision.HIGHEST
    )
    slot_norms = jnp.zeros((columns * lax.axis_size("sa"),), jnp.float32)
    slot_norms = lax.dynamic_update_slice_in_dim(
        slot_norms, partial_value, lax.axis_index("sa") * columns, 0
    )
    raw_gram, totals = lax.psum((gram_local, slot_norms), ("gx", "gz", "sa"))
    scale_all = jnp.sqrt(totals / entries + 1e-06)
    gram = raw_gram / entries / (scale_all[:, None] * scale_all[None, :])
    factor = upper_factor(gram)
    inverse = upper_inverse(factor)
    coefficient = inverse / scale_all[:, None]
    own_coef = lax.dynamic_slice_in_dim(coefficient, lax.axis_index("sa") * columns, columns, 1)
    basis_own = jnp.einsum("cixzy,ij->cjxzy", gathered, own_coef, precision=lax.Precision.HIGHEST)
    return (basis_own, factor)


def solution(mesh):
    return jax.shard_map(
        shards,
        mesh=mesh,
        in_specs=(P(None, "sa", "gx", "gz", None), P(), P()),
        out_specs=(P(None, "sa", "gx", "gz", None), P()),
        check_vma=False,
    )
```

profile of v0, /device:TPU:0, one launch (start us, length us, event | category | flops | bytes accessed | tf_op | source)
XLA Modules:
  0.0 341.3 jit_solution(7292808118564609644)
XLA Ops:
  8.2 3.1 collective-permute-start.1
  14.2 2.5 collective-permute-done.1
  22.2 6.5 %collective-permute-done.2 = f32[3,4,34,1,256]{4,3,2,1,0:T(1,128)S(1)} collective-permute-done((f32[3,4,34,1,256]{4,3,2,1,0:T(1,128)S(1)}, f32[3,4,34,1,256]{4,3,2,1,0:T(1,128)S(1)}, u32[]{:S(2)}, u32[]{:S(2)}) %collective-permute-start.2) | collective-permute-done | bytes 417824 | tf_op jit(solution)/shard_map/ppermute | solution.py:19
  28.7 3.0 collective-permute-done.3
  34.2 2.8 fusion.32
  37.0 3.4 collective-permute-start.4
  40.4 3.2 collective-permute-done.4
  43.6 3.2 collective-permute-done.5
  47.9 9.3 %collective-permute-done.6 = f32[3,4,34,1,256]{4,3,2,1,0:T(1,128)S(1)} collective-permute-done((f32[3,4,34,1,256]{4,3,2,1,0:T(1,128)S(1)}, f32[3,4,34,1,256]{4,3,2,1,0:T(1,128)S(1)}, u32[]{:S(2)}, u32[]{:S(2)}) %collective-permute-start.6) | collective-permute-done | bytes 417824 | tf_op jit(solution)/shard_map/ppermute | solution.py:19
  58.4 2.4 fusion.15
  61.1 2.9 fusion.28
  64.0 2.8 fusion.54
  69.0 3.6 %collective-permute-done.8 = f32[3,4,1,8,256]{4,3,2,1,0:T(8,128)S(1)} collective-permute-done((f32[3,4,1,8,256]{4,3,2,1,0:T(8,128)S(1)}, f32[3,4,1,8,256]{4,3,2,1,0:T(8,128)S(1)}, u32[]{:S(2)}, u32[]{:S(2)}) %collective-permute-start.8) | collective-permute-done | bytes 98336 | tf_op jit(solution)/shard_map/ppermute | solution.py:19
  75.1 8.5 %collective-permute-done.10 = f32[3,4,34,1,256]{4,3,2,1,0:T(1,128)S(1)} collective-permute-done((f32[3,4,34,1,256]{4,3,2,1,0:T(1,128)S(1)}, f32[3,4,34,1,256]{4,3,2,1,0:T(1,128)S(1)}, u32[]{:S(2)}, u32[]{:S(2)}) %collective-permute-start.10) | collective-permute-done | bytes 417824 | tf_op jit(solution)/shard_map/ppermute | solution.py:19
  83.5 3.0 collective-permute-done.11
  89.2 3.0 fusion.24
  94.2 2.8 collective-permute-done.12
  97.0 2.6 collective-permute-done.13
  100.8 9.1 %collective-permute-done.14 = f32[3,4,34,1,256]{4,3,2,1,0:T(1,128)S(1)} collective-permute-done((f32[3,4,34,1,256]{4,3,2,1,0:T(1,128)S(1)}, f32[3,4,34,1,256]{4,3,2,1,0:T(1,128)S(1)}, u32[]{:S(2)}, u32[]{:S(2)}) %collective-permute-start.14) | collective-permute-done | bytes 417824 | tf_op jit(solution)/shard_map/ppermute | solution.py:19
  109.9 2.4 collective-permute-done.15
  112.3 2.4 fusion.5
  115.0 2.5 multiply_reduce_fusion
  117.9 78.3 %all-gather.2.cloned.1.call-done = f32[3,8,32,8,256]{4,3,2,1,0:T(8,128)} async-done(((f32[3,4,32,8,256]{4,3,2,1,0:T(8,128)}), f32[3,8,32,8,256]{4,3,2,1,0:T(8,128)}) %all-gather.2.cloned.1.call-update) | async-done | bytes 6291472 | tf_op jit(solution)/shard_map/all_gather | solution.py:109
  198.2 7.5 %fusion.43 = f32[8,8]{1,0:T(8,128)S(1)} fusion(f32[3,8,32,8,128]{4,3,2,1,0:T(8,128)S(1)} %constant_dynamic-slice_fusion), kind=kOutput, calls=%fused_computation.71 | convolution fusion | flops 75497472 | bytes 3145984 | tf_op jit(solution)/shard_map/cixzy,cjxzy->ij/dot_general | solution.py:112
  205.7 39.6 %all-reduce = (f32[8,8]{1,0:T(8,128)S(1)}, f32[8]{0:T(128)S(1)}) all-reduce(f32[8,8]{1,0:T(8,128)S(1)} %fusion.43, f32[8]{0:T(128)S(1)} %dynamic_update_slice.3), channel_id=1, replica_groups=mesh['gx'=4,'gz'=4,'sa'=2] {'gx','gz','sa'}, use_global_device_ids=true, to_apply=%region_0.0 | all-reduce | flops 72 | bytes 576 | tf_op jit(solution)/shard_map/psum | solution.py:119
  257.0 2.5 fusion.85
  261.5 3.1 fusion.83
  266.5 3.8 %multiply_subtract_fusion.2 = f32[8]{0:T(128)S(1)} fusion(f32[]{:T(128)} %bitcast.40, f32[]{:T(128)} %bitcast.39, f32[]{:T(128)} %bitcast.38, f32[]{:T(128)} %bitcast.37, f32[]{:T(128)} %bitcast.36, f32[]{:T(128)} %bitcast.35, f32[8,8]{1,0:T(8,128)S(1)} %multiply_divide_fusion, f32[]{:T(128)} %bitcast.33, f32[8]{0:T(128)S(1)} %fusion.83, f32[]{:T(128)} %bitcast.25, ...), kind=kLoop, calls=%fused_computation.164 | loop fusion | flops 224 | bytes 304 | tf_op jit(solution)/shard_map/sub | solution.py:38
  272.3 4.6 %multiply_subtract_fusion = f32[8]{0:T(128)S(1)} fusion(f32[]{:T(128)} %bitcast.50, f32[]{:T(128)} %bitcast.49, f32[]{:T(128)} %bitcast.48, f32[]{:T(128)} %bitcast.47, f32[]{:T(128)} %bitcast.46, f32[]{:T(128)} %bitcast.45, f32[]{:T(128)} %bitcast.44, f32[8,8]{1,0:T(8,128)S(1)} %multiply_divide_fusion, f32[]{:T(128)} %bitcast.42, ...), kind=kLoop, calls=%fused_computation.161 | loop fusion | flops 264 | bytes 344 | tf_op jit(solution)/shard_map/sub | solution.py:38
  278.1 16.9 %fusion.73 = (f32[1,8]{1,0:T(1,128)S(1)}, f32[1,8]{1,0:T(1,128)S(1)}, f32[1,8]{1,0:T(1,128)S(1)}, f32[1,8]{1,0:T(1,128)S(1)}, f32[1,8]{1,0:T(1,128)S(1)}, /*index=5*/f32[1,8]{1,0:T(1,128)S(1)}, f32[1,8]{1,0:T(1,128)S(1)}) fusion(f32[]{:T(128)} %bitcast.52, f32[]{:T(128)} %bitcast.50, f32[]{:T(128)} %bitcast.49, f32[]{:T(128)} %bitcast.48, f32[]{:T(128)} %bitcast.47, ...), kind=kLoop, calls=%fused_computation.134 | loop fusion | flops 608 | bytes 620 | tf_op jit(solution)/shard_map/div | solution.py:39
  298.3 22.7 %subtract_divide_fusion = (f32[1,8]{1,0:T(1,128)S(1)}, f32[1,8]{1,0:T(1,128)S(1)}, f32[1,8]{1,0:T(1,128)S(1)}, f32[1,8]{1,0:T(1,128)S(1)}, f32[1,8]{1,0:T(1,128)...) fusion(f32[8,8]{1,0:T(8,128)S(1)} %fusion.60, f32[]{:T(128)} %bitcast.75, f32[]{:T(128)} %bitcast.44, ...), kind=kLoop, calls=%fused_computation.154 | loop fusion | flops 512 | bytes 656 | tf_op jit(solution)/shard_map/div | solution.py:54
  321.1 11.2 %fusion.37 = f32[3,4,32,8,256]{4,1,3,2,0:T(4,128)S(1)} fusion(f32[3,8,32,8,256]{4,3,2,1,0:T(8,128)} %all-gather.2.cloned.1.call-done, f32[8,8]{1,0:T(8,128)S(1)} %broadcast_divide_fusion, s32[]{:T(128)S(6)} %select_n.71), kind=kOutput, calls=%fused_computation.67 | convolution fusion | flops 75497472 | bytes 9437444 | tf_op jit(solution)/shard_map/cixzy,ij->cjxzy/dot_general | solution.py:126
  (85 shorter events, 46.2 us)
Async XLA Ops:
  7.2 27.0 %copy-start = (f32[256,256]{1,0:T(8,128)S(1)}, f32[256,256]{1,0:T(8,128)}, u32[]{:S(2)}) copy-start(f32[256,256]{1,0:T(8,128)} %param.13) | copy-start | bytes 786436
  7.2 188.9 %all-gather.2.cloned.1.call-start = ((), (), s32[]{:S(2)}) async-start(), calls=%async_computation | async-start | bytes 9437184 | tf_op jit(solution)/shard_map/all_gather | solution.py:109
  8.2 8.6 %collective-permute-start.1 = (f32[3,4,1,8,256]{4,3,2,1,0:T(8,128)S(1)}, f32[3,4,1,8,256]{4,3,2,1,0:T(8,128)S(1)}, u32[]{:S(2)}, u32[]{:S(2)}) collective-permute-start(f32[3,4,1,8,256]{4,3,2,1,0:T(8,128)S(1)} %get-tuple-element.86), channel_id=1, source_target_pairs={{0,8},{8,16},{16,24},{24,0},{1,9},{9,17},{17,25},{25,1},{2,10},{10... | collective-permute-start | bytes 294920 | tf_op jit(solution)/shard_map/ppermute | solution.py:17
  11.3 7.8 %collective-permute-start = (f32[3,4,1,8,256]{4,3,2,1,0:T(8,128)S(1)}, f32[3,4,1,8,256]{4,3,2,1,0:T(8,128)S(1)}, u32[]{:S(2)}, u32[]{:S(2)}) collective-permute-start(f32[3,4,1,8,256]{4,3,2,1,0:T(8,128)S(1)} %get-tuple-element.85), channel_id=1, source_target_pairs={{8,0},{16,8},{24,16},{0,24},{9,1},{17,9},{25,17},{1,25},{10,2},{18... | collective-permute-start | bytes 294920 | tf_op jit(solution)/shard_map/ppermute | solution.py:19
  16.8 3.4 copy-start.2
  16.8 14.8 %copy-start.1 = (f32[3,4,32,8,256]{4,3,2,1,0:T(8,128)S(1)}, f32[3,4,32,8,256]{4,3,2,1,0:T(8,128)}, u32[]{:S(2)}) copy-start(f32[3,4,32,8,256]{4,3,2,1,0:T(8,128)} %param.11) | copy-start | bytes 9437188
  19.6 9.0 %collective-permute-start.2 = (f32[3,4,34,1,256]{4,3,2,1,0:T(1,128)S(1)}, f32[3,4,34,1,256]{4,3,2,1,0:T(1,128)S(1)}, u32[]{:S(2)}, u32[]{:S(2)}) collective-permute-start(f32[3,4,34,1,256]{4,3,2,1,0:T(1,128)S(1)} %get-tuple-element.75), channel_id=1, source_target_pairs={{2,0},{4,2},{6,4},{0,6},{3,1},{5,3},{7,5},{1,7},{10,8},{12,10},{14... | collective-permute-start | bytes 1253384 | tf_op jit(solution)/shard_map/ppermute | solution.py:19
  19.7 11.9 %collective-permute-start.3 = (f32[3,4,34,1,256]{4,3,2,1,0:T(1,128)S(1)}, f32[3,4,34,1,256]{4,3,2,1,0:T(1,128)S(1)}, u32[]{:S(2)}, u32[]{:S(2)}) collective-permute-start(f32[3,4,34,1,256]{4,3,2,1,0:T(1,128)S(1)} %get-tuple-element.76), channel_id=1, source_target_pairs={{0,2},{2,4},{4,6},{6,0},{1,3},{3,5},{5,7},{7,1},{8,10},{10,12},{12... | collective-permute-start | bytes 1253384 | tf_op jit(solution)/shard_map/ppermute | solution.py:17
  37.0 6.6 %collective-permute-start.4 = (f32[3,4,1,8,256]{4,3,2,1,0:T(8,128)S(1)}, f32[3,4,1,8,256]{4,3,2,1,0:T(8,128)S(1)}, u32[]{:S(2)}, u32[]{:S(2)}) collective-permute-start(f32[3,4,1,8,256]{4,3,2,1,0:T(8,128)S(1)} %get-tuple-element.84), channel_id=1, source_target_pairs={{8,0},{16,8},{24,16},{0,24},{9,1},{17,9},{25,17},{1,25},{10,2},{18... | collective-permute-start | bytes 294920 | tf_op jit(solution)/shard_map/ppermute | solution.py:19
  40.4 6.4 %collective-permute-start.5 = (f32[3,4,1,8,256]{4,3,2,1,0:T(8,128)S(1)}, f32[3,4,1,8,256]{4,3,2,1,0:T(8,128)S(1)}, u32[]{:S(2)}, u32[]{:S(2)}) collective-permute-start(f32[3,4,1,8,256]{4,3,2,1,0:T(8,128)S(1)} %get-tuple-element.83), channel_id=1, source_target_pairs={{0,8},{8,16},{16,24},{24,0},{1,9},{9,17},{17,25},{25,1},{2,10},{10... | collective-permute-start | bytes 294920 | tf_op jit(solution)/shard_map/ppermute | solution.py:17
  47.3 9.9 %collective-permute-start.6 = (f32[3,4,34,1,256]{4,3,2,1,0:T(1,128)S(1)}, f32[3,4,34,1,256]{4,3,2,1,0:T(1,128)S(1)}, u32[]{:S(2)}, u32[]{:S(2)}) collective-permute-start(f32[3,4,34,1,256]{4,3,2,1,0:T(1,128)S(1)} %get-tuple-element.73), channel_id=1, source_target_pairs={{2,0},{4,2},{6,4},{0,6},{3,1},{5,3},{7,5},{1,7},{10,8},{12,10},{14... | collective-permute-start | bytes 1253384 | tf_op jit(solution)/shard_map/ppermute | solution.py:19
  47.4 11.0 %collective-permute-start.7 = (f32[3,4,34,1,256]{4,3,2,1,0:T(1,128)S(1)}, f32[3,4,34,1,256]{4,3,2,1,0:T(1,128)S(1)}, u32[]{:S(2)}, u32[]{:S(2)}) collective-permute-start(f32[3,4,34,1,256]{4,3,2,1,0:T(1,128)S(1)} %get-tuple-element.74), channel_id=1, source_target_pairs={{0,2},{2,4},{4,6},{6,0},{1,3},{3,5},{5,7},{7,1},{8,10},{10,12},{12... | collective-permute-start | bytes 1253384 | tf_op jit(solution)/shard_map/ppermute | solution.py:17
  66.9 5.7 %collective-permute-start.8 = (f32[3,4,1,8,256]{4,3,2,1,0:T(8,128)S(1)}, f32[3,4,1,8,256]{4,3,2,1,0:T(8,128)S(1)}, u32[]{:S(2)}, u32[]{:S(2)}) collective-permute-start(f32[3,4,1,8,256]{4,3,2,1,0:T(8,128)S(1)} %get-tuple-element.82), channel_id=1, source_target_pairs={{8,0},{16,8},{24,16},{0,24},{9,1},{17,9},{25,17},{1,25},{10,2},{18... | collective-permute-start | bytes 294920 | tf_op jit(solution)/shard_map/ppermute | solution.py:19
  67.5 6.5 %collective-permute-start.9 = (f32[3,4,1,8,256]{4,3,2,1,0:T(8,128)S(1)}, f32[3,4,1,8,256]{4,3,2,1,0:T(8,128)S(1)}, u32[]{:S(2)}, u32[]{:S(2)}) collective-permute-start(f32[3,4,1,8,256]{4,3,2,1,0:T(8,128)S(1)} %get-tuple-element.81), channel_id=1, source_target_pairs={{0,8},{8,16},{16,24},{24,0},{1,9},{9,17},{17,25},{25,1},{2,10},{10... | collective-permute-start | bytes 294920 | tf_op jit(solution)/shard_map/ppermute | solution.py:17
  74.5 9.0 %collective-permute-start.10 = (f32[3,4,34,1,256]{4,3,2,1,0:T(1,128)S(1)}, f32[3,4,34,1,256]{4,3,2,1,0:T(1,128)S(1)}, u32[]{:S(2)}, u32[]{:S(2)}) collective-permute-start(f32[3,4,34,1,256]{4,3,2,1,0:T(1,128)S(1)} %get-tuple-element.71), channel_id=1, source_target_pairs={{2,0},{4,2},{6,4},{0,6},{3,1},{5,3},{7,5},{1,7},{10,8},{12,10},{14... | collective-permute-start | bytes 1253384 | tf_op jit(solution)/shard_map/ppermute | solution.py:19
  74.6 11.9 %collective-permute-start.11 = (f32[3,4,34,1,256]{4,3,2,1,0:T(1,128)S(1)}, f32[3,4,34,1,256]{4,3,2,1,0:T(1,128)S(1)}, u32[]{:S(2)}, u32[]{:S(2)}) collective-permute-start(f32[3,4,34,1,256]{4,3,2,1,0:T(1,128)S(1)} %get-tuple-element.72), channel_id=1, source_target_pairs={{0,2},{2,4},{4,6},{6,0},{1,3},{3,5},{5,7},{7,1},{8,10},{10,12},{12... | collective-permute-start | bytes 1253384 | tf_op jit(solution)/shard_map/ppermute | solution.py:17
  92.2 4.9 %collective-permute-start.12 = (f32[3,4,1,8,256]{4,3,2,1,0:T(8,128)S(1)}, f32[3,4,1,8,256]{4,3,2,1,0:T(8,128)S(1)}, u32[]{:S(2)}, u32[]{:S(2)}) collective-permute-start(f32[3,4,1,8,256]{4,3,2,1,0:T(8,128)S(1)} %get-tuple-element.80), channel_id=1, source_target_pairs={{8,0},{16,8},{24,16},{0,24},{9,1},{17,9},{25,17},{1,25},{10,2},{18... | collective-permute-start | bytes 294920 | tf_op jit(solution)/shard_map/ppermute | solution.py:19
  93.1 6.6 %collective-permute-start.13 = (f32[3,4,1,8,256]{4,3,2,1,0:T(8,128)S(1)}, f32[3,4,1,8,256]{4,3,2,1,0:T(8,128)S(1)}, u32[]{:S(2)}, u32[]{:S(2)}) collective-permute-start(f32[3,4,1,8,256]{4,3,2,1,0:T(8,128)S(1)} %get-tuple-element.79), channel_id=1, source_target_pairs={{0,8},{8,16},{16,24},{24,0},{1,9},{9,17},{17,25},{25,1},{2,10},{10... | collective-permute-start | bytes 294920 | tf_op jit(solution)/shard_map/ppermute | solution.py:17
  100.2 9.7 %collective-permute-start.14 = (f32[3,4,34,1,256]{4,3,2,1,0:T(1,128)S(1)}, f32[3,4,34,1,256]{4,3,2,1,0:T(1,128)S(1)}, u32[]{:S(2)}, u32[]{:S(2)}) collective-permute-start(f32[3,4,34,1,256]{4,3,2,1,0:T(1,128)S(1)} %get-tuple-element.69), channel_id=1, source_target_pairs={{2,0},{4,2},{6,4},{0,6},{3,1},{5,3},{7,5},{1,7},{10,8},{12,10},{14... | collective-permute-start | bytes 1253384 | tf_op jit(solution)/shard_map/ppermute | solution.py:19
  100.6 11.7 %collective-permute-start.15 = (f32[3,4,34,1,256]{4,3,2,1,0:T(1,128)S(1)}, f32[3,4,34,1,256]{4,3,2,1,0:T(1,128)S(1)}, u32[]{:S(2)}, u32[]{:S(2)}) collective-permute-start(f32[3,4,34,1,256]{4,3,2,1,0:T(1,128)S(1)} %get-tuple-element.70), channel_id=1, source_target_pairs={{0,2},{2,4},{4,6},{6,0},{1,3},{3,5},{5,7},{7,1},{8,10},{10,12},{12... | collective-permute-start | bytes 1253384 | tf_op jit(solution)/shard_map/ppermute | solution.py:17
Sparse Core Ops, SparseCore 0:
  117.7 78.3 all-gather.1
where the time goes:
time: 342 us; the launch traced here: 341 us
  waiting for transfers between devices  141 us (41%)
  other arithmetic  74.8 us (22%)
  blocking collectives  39.6 us (12%)
  matrix products  30.2 us (9%)
  local copies, waits for them, and re-layouts  21.2 us (6%)
  between operations  19.9 us (6%)
  starting transfers between devices  15 us (4%)
    all_gather x1, waiting for transfers between devices, shards(): gathered = lax.all_gather(current, 'sa', axis=1, tiled=True)  78.3 us
    ppermute x8, waiting for transfers between devices, extended(): lax.ppermute(head, axis, [((i + 1) % count, i) for i in range(count)])  43.1 us
    psum x1, blocking collectives, shards(): raw_gram, totals = lax.psum((gram_local, slot_norms), ('gx', 'gz', 'sa'))  39.6 us
    div x1, other arithmetic, upper_inverse(): row_list[pivot_index] = current_row / factor[pivot_index, pivot_index]  22.7 us
    ppermute x8, waiting for transfers between devices, extended(): lax.ppermute(tail, axis, [(i, (i + 1) % count) for i in range(count)])  19.3 us
    sub x7, other arithmetic, upper_factor(): current_row - row_list[other_index][pivot_index] * row_list[other_index]  17.6 us
    div x8, other arithmetic, upper_factor(): jnp.where(column_ids >= pivot_index, current_row, jnp.zeros_like(current_...  17 us
    dot_general x1, matrix products, shards(): jnp.einsum('cixzy,ij->cjxzy', gathered, own_coef, precision=lax.Precision...  11.2 us
  transfers between devices with their start and end apart: 17, of which 16 were waited for; matrix products, arithmetic and copies ran while one was open for 2% of the time, Pallas kernels for 0%

commit v1 on v0

--- a/solution.py
+++ b/solution.py
@@ -106,7 +106,14 @@
         solved = wall_adjoint(current, wall_solve)
         center, change = stencil(near_faces(solved), velocity, shear_rate, True)
         current = center + step_length * change + step_length * response
-    gathered = lax.all_gather(current, "sa", axis=1, tiled=True)
+    ways, here, lap = (lax.axis_size("sa"), lax.axis_index("sa"), current.shape[1])
+    line, have = (current, 1)
+    while have < ways:
+        line = jnp.concatenate(
+            [line, lax.ppermute(line, "sa", [(d, (d - have) % ways) for d in range(ways)])], axis=1
+        )
+        have = 2 * have
+    gathered = jnp.roll(line, here * lap, axis=1)
     half_rows = gathered.shape[4] // lax.axis_size("sa")
     row_block = lax.dynamic_slice_in_dim(gathered, lax.axis_index("sa") * half_rows, half_rows, 4)
     gram_local = jnp.einsum(

time: 342 us -> 330 us (0.965)
  between operations: 19.9 us -> 6.12 us
  waiting for transfers between devices: 141 us -> 131 us
  local copies, waits for them, and re-layouts: 21.2 us -> 30 us
    all_gather x1 -> x0, waiting for transfers between devices: 78.3 us -> none  [shards(): gathered = lax.all_gather(current, 'sa', axis=1, tiled=True)]
    ppermute x0 -> x1, waiting for transfers between devices: none -> 68.3 us  [shards(): lax.ppermute(line, 'sa', [(d, (d - have) % ways) for d in range(ways)])]
    dynamic_slice x0 -> x1, local copies, waits for them, and re-layouts: none -> 6.01 us  [shards(): gathered = jnp.roll(line, here * lap, axis=1)]
    concatenate x0 -> x1, other arithmetic: none -> 4.7 us  [shards(): gathered = jnp.roll(line, here * lap, axis=1)]
    unnamed x9 -> x13, local copies, waits for them, and re-layouts: 4.5 us -> 9.01 us
where the time goes in v1:
time: 330 us; the launch traced here: 329 us
  waiting for transfers between devices  131 us (40%)
  other arithmetic  77.1 us (23%)
  blocking collectives  38.2 us (12%)
  matrix products  30.3 us (9%)
  local copies, waits for them, and re-layouts  30 us (9%)
  starting transfers between devices  16.5 us (5%)
  between operations  6.12 us (2%)
    ppermute x1, waiting for transfers between devices, shards(): lax.ppermute(line, 'sa', [(d, (d - have) % ways) for d in range(ways)])  68.3 us
    ppermute x8, waiting for transfers between devices, extended(): lax.ppermute(head, axis, [((i + 1) % count, i) for i in range(count)])  43.1 us
    psum x1, blocking collectives, shards(): raw_gram, totals = lax.psum((gram_local, slot_norms), ('gx', 'gz', 'sa'))  38.2 us
    div x1, other arithmetic, upper_inverse(): row_list[pivot_index] = current_row / factor[pivot_index, pivot_index]  22.2 us
    ppermute x8, waiting for transfers between devices, extended(): lax.ppermute(tail, axis, [(i, (i + 1) % count) for i in range(count)])  19.3 us
    sub x7, other arithmetic, upper_factor(): current_row - row_list[other_index][pivot_index] * row_list[other_index]  17.5 us
    div x8, other arithmetic, upper_factor(): jnp.where(column_ids >= pivot_index, current_row, jnp.zeros_like(current_...  16.8 us
    dot_general x1, matrix products, shards(): jnp.einsum('cixzy,ij->cjxzy', gathered, own_coef, precision=lax.Precision...  11.3 us
  transfers between devices with their start and end apart: 17, of which 16 were waited for; matrix products, arithmetic and copies ran while one was open for 2% of the time, Pallas kernels for 0%

profile of v1, /device:TPU:0, one launch (start us, length us, event | category | flops | bytes accessed | tf_op | source)
XLA Modules:
  0.0 329.0 jit_solution(12279312556103069162)
XLA Ops:
  1.6 3.1 collective-permute-start.1
  7.7 2.5 collective-permute-done.1
  15.6 6.5 %collective-permute-done.2 = f32[3,4,34,1,256]{4,3,2,1,0:T(1,128)S(1)} collective-permute-done((f32[3,4,34,1,256]{4,3,2,1,0:T(1,128)S(1)}, f32[3,4,34,1,256]{4,3,2,1,0:T(1,128)S(1)}, u32[]{:S(2)}, u32[]{:S(2)}) %collective-permute-start.2) | collective-permute-done | bytes 417824 | tf_op jit(solution)/shard_map/ppermute | solution.py:19
  22.1 3.0 collective-permute-done.3
  27.6 2.8 fusion.32
  30.5 3.4 %collective-permute-start.4 = (f32[3,4,1,8,256]{4,3,2,1,0:T(8,128)S(1)}, f32[3,4,1,8,256]{4,3,2,1,0:T(8,128)S(1)}, u32[]{:S(2)}, u32[]{:S(2)}) collective-permute-start(f32[3,4,1,8,256]{4,3,2,1,0:T(8,128)S(1)} %get-tuple-element.84), channel_id=1, source_target_pairs={{8,0},{16,8},{24,16},{0,24},{9,1},{17,9},{25,17},{1,25},{10,2},{18... | collective-permute-start | bytes 294920 | tf_op jit(solution)/shard_map/ppermute | solution.py:19
  33.9 3.2 collective-permute-done.4
  37.0 3.2 collective-permute-done.5
  41.3 9.3 %collective-permute-done.6 = f32[3,4,34,1,256]{4,3,2,1,0:T(1,128)S(1)} collective-permute-done((f32[3,4,34,1,256]{4,3,2,1,0:T(1,128)S(1)}, f32[3,4,34,1,256]{4,3,2,1,0:T(1,128)S(1)}, u32[]{:S(2)}, u32[]{:S(2)}) %collective-permute-start.6) | collective-permute-done | bytes 417824 | tf_op jit(solution)/shard_map/ppermute | solution.py:19
  54.6 2.9 fusion.28
  57.5 2.8 fusion.54
  62.4 3.6 %collective-permute-done.8 = f32[3,4,1,8,256]{4,3,2,1,0:T(8,128)S(1)} collective-permute-done((f32[3,4,1,8,256]{4,3,2,1,0:T(8,128)S(1)}, f32[3,4,1,8,256]{4,3,2,1,0:T(8,128)S(1)}, u32[]{:S(2)}, u32[]{:S(2)}) %collective-permute-start.8) | collective-permute-done | bytes 98336 | tf_op jit(solution)/shard_map/ppermute | solution.py:19
  68.5 8.5 %collective-permute-done.10 = f32[3,4,34,1,256]{4,3,2,1,0:T(1,128)S(1)} collective-permute-done((f32[3,4,34,1,256]{4,3,2,1,0:T(1,128)S(1)}, f32[3,4,34,1,256]{4,3,2,1,0:T(1,128)S(1)}, u32[]{:S(2)}, u32[]{:S(2)}) %collective-permute-start.10) | collective-permute-done | bytes 417824 | tf_op jit(solution)/shard_map/ppermute | solution.py:19
  76.9 3.0 collective-permute-done.11
  82.6 3.0 fusion.24
  87.7 2.8 collective-permute-done.12
  90.5 2.7 collective-permute-done.13
  94.2 9.1 %collective-permute-done.14 = f32[3,4,34,1,256]{4,3,2,1,0:T(1,128)S(1)} collective-permute-done((f32[3,4,34,1,256]{4,3,2,1,0:T(1,128)S(1)}, f32[3,4,34,1,256]{4,3,2,1,0:T(1,128)S(1)}, u32[]{:S(2)}, u32[]{:S(2)}) %collective-permute-start.14) | collective-permute-done | bytes 417824 | tf_op jit(solution)/shard_map/ppermute | solution.py:19
  103.3 2.4 collective-permute-done.15
  111.1 68.3 %collective-permute-done.16 = f32[3,4,32,8,256]{4,3,2,1,0:T(8,128)} collective-permute-done((f32[3,4,32,8,256]{4,3,2,1,0:T(8,128)S(1)}, f32[3,4,32,8,256]{4,3,2,1,0:T(8,128)}, u32[]{:S(2)}, u32[]{:S(2)}) %collective-permute-start.16) | collective-permute-done | bytes 3145760 | tf_op jit(solution)/shard_map/ppermute | solution.py:113
  179.4 4.7 %pad_maximum_fusion = f32[3,16,32,8,256]{4,3,2,1,0:T(8,128)S(1)} fusion(f32[3,4,32,8,256]{4,3,2,1,0:T(8,128)} %collective-permute-done.16, f32[3,4,32,8,256]{4,3,2,1,0:T(8,128)S(1)} %get-tuple-element.78), kind=kLoop, calls=%fused_computation | loop fusion | flops 9437184 | bytes 18874368 | tf_op jit(solution)/shard_map/jit(_roll_dynamic)/concatenate | solution.py:116
  184.1 4.5 %copy-done.3 = f32[3,16,32,8,256]{4,3,2,1,0:T(8,128)} copy-done((f32[3,16,32,8,256]{4,3,2,1,0:T(8,128)}, f32[3,16,32,8,256]{4,3,2,1,0:T(8,128)S(1)}, u32[]{:S(2)}) %copy-start.3) | copy-done | bytes 12582936
  189.5 7.5 %fusion.43 = f32[8,8]{1,0:T(8,128)S(1)} fusion(f32[3,8,32,8,128]{4,3,2,1,0:T(8,128)S(1)} %constant_dynamic-slice_fusion.1), kind=kOutput, calls=%fused_computation.72 | convolution fusion | flops 75497472 | bytes 3145984 | tf_op jit(solution)/shard_map/cixzy,cjxzy->ij/dot_general | solution.py:119
  197.0 38.2 %all-reduce = (f32[8,8]{1,0:T(8,128)S(1)}, f32[8]{0:T(128)S(1)}) all-reduce(f32[8,8]{1,0:T(8,128)S(1)} %fusion.43, f32[8]{0:T(128)S(1)} %dynamic_update_slice.3), channel_id=1, replica_groups=mesh['gx'=4,'gz'=4,'sa'=2] {'gx','gz','sa'}, use_global_device_ids=true, to_apply=%region_0.0 | all-reduce | flops 72 | bytes 576 | tf_op jit(solution)/shard_map/psum | solution.py:126
  246.8 2.6 fusion.85
  251.3 3.2 fusion.83
  256.3 3.7 %multiply_subtract_fusion.2 = f32[8]{0:T(128)S(1)} fusion(f32[]{:T(128)} %bitcast.40, f32[]{:T(128)} %bitcast.39, f32[]{:T(128)} %bitcast.38, f32[]{:T(128)} %bitcast.37, f32[]{:T(128)} %bitcast.36, f32[]{:T(128)} %bitcast.35, f32[8,8]{1,0:T(8,128)S(1)} %multiply_divide_fusion, f32[]{:T(128)} %bitcast.33, f32[8]{0:T(128)S(1)} %fusion.83, f32[]{:T(128)} %bitcast.25, ...), kind=kLoop, calls=%fused_computation.166 | loop fusion | flops 224 | bytes 304 | tf_op jit(solution)/shard_map/sub | solution.py:38
  261.7 4.2 %multiply_subtract_fusion = f32[8]{0:T(128)S(1)} fusion(f32[]{:T(128)} %bitcast.50, f32[]{:T(128)} %bitcast.49, f32[]{:T(128)} %bitcast.48, f32[]{:T(128)} %bitcast.47, f32[]{:T(128)} %bitcast.46, f32[]{:T(128)} %bitcast.45, f32[]{:T(128)} %bitcast.44, f32[8,8]{1,0:T(8,128)S(1)} %multiply_divide_fusion, f32[]{:T(128)} %bitcast.42, ...), kind=kLoop, calls=%fused_computation.163 | loop fusion | flops 264 | bytes 344 | tf_op jit(solution)/shard_map/sub | solution.py:38
  267.1 16.8 %fusion.73 = (f32[1,8]{1,0:T(1,128)S(1)}, f32[1,8]{1,0:T(1,128)S(1)}, f32[1,8]{1,0:T(1,128)S(1)}, f32[1,8]{1,0:T(1,128)S(1)}, f32[1,8]{1,0:T(1,128)S(1)}, /*index=5*/f32[1,8]{1,0:T(1,128)S(1)}, f32[1,8]{1,0:T(1,128)S(1)}) fusion(f32[]{:T(128)} %bitcast.52, f32[]{:T(128)} %bitcast.50, f32[]{:T(128)} %bitcast.49, f32[]{:T(128)} %bitcast.48, f32[]{:T(128)} %bitcast.47, ...), kind=kLoop, calls=%fused_computation.136 | loop fusion | flops 608 | bytes 620 | tf_op jit(solution)/shard_map/div | solution.py:39
  287.1 6.0 %constant_dynamic-slice_fusion = f32[3,8,32,8,256]{4,3,2,1,0:T(8,128)} fusion(f32[3,16,32,8,256]{4,3,2,1,0:T(8,128)} %copy-done.3, s32[]{:T(128)S(6)} %select_n.88), kind=kLoop, calls=%fused_computation.120 | loop fusion | bytes 12582916 | tf_op jit(solution)/shard_map/jit(_roll_dynamic)/dynamic_slice | solution.py:116
  293.1 22.2 %subtract_divide_fusion = (f32[1,8]{1,0:T(1,128)S(1)}, f32[1,8]{1,0:T(1,128)S(1)}, f32[1,8]{1,0:T(1,128)S(1)}, f32[1,8]{1,0:T(1,128)S(1)}, f32[1,8]{1,0:T(1,128)...) fusion(f32[8,8]{1,0:T(8,128)S(1)} %fusion.60, f32[]{:T(128)} %bitcast.75, f32[]{:T(128)} %bitcast.44, ...), kind=kLoop, calls=%fused_computation.156 | loop fusion | flops 512 | bytes 656 | tf_op jit(solution)/shard_map/div | solution.py:54
  315.5 11.3 %fusion.37 = f32[3,4,32,8,256]{4,1,3,2,0:T(4,128)S(1)} fusion(f32[3,8,32,8,256]{4,3,2,1,0:T(8,128)} %constant_dynamic-slice_fusion, f32[8,8]{1,0:T(8,128)S(1)} %broadcast_divide_fusion, s32[]{:T(128)S(6)} %select_n.92), kind=kOutput, calls=%fused_computation.68 | convolution fusion | flops 75497472 | bytes 9437444 | tf_op jit(solution)/shard_map/cixzy,ij->cjxzy/dot_general | solution.py:133
  (90 shorter events, 51.8 us)
Async XLA Ops:
  0.6 27.0 %copy-start = (f32[256,256]{1,0:T(8,128)S(1)}, f32[256,256]{1,0:T(8,128)}, u32[]{:S(2)}) copy-start(f32[256,256]{1,0:T(8,128)} %param.13) | copy-start | bytes 786436
  1.6 8.6 %collective-permute-start.1 = (f32[3,4,1,8,256]{4,3,2,1,0:T(8,128)S(1)}, f32[3,4,1,8,256]{4,3,2,1,0:T(8,128)S(1)}, u32[]{:S(2)}, u32[]{:S(2)}) collective-permute-start(f32[3,4,1,8,256]{4,3,2,1,0:T(8,128)S(1)} %get-tuple-element.86), channel_id=1, source_target_pairs={{0,8},{8,16},{16,24},{24,0},{1,9},{9,17},{17,25},{25,1},{2,10},{10... | collective-permute-start | bytes 294920 | tf_op jit(solution)/shard_map/ppermute | solution.py:17
  4.8 7.8 %collective-permute-start = (f32[3,4,1,8,256]{4,3,2,1,0:T(8,128)S(1)}, f32[3,4,1,8,256]{4,3,2,1,0:T(8,128)S(1)}, u32[]{:S(2)}, u32[]{:S(2)}) collective-permute-start(f32[3,4,1,8,256]{4,3,2,1,0:T(8,128)S(1)} %get-tuple-element.85), channel_id=1, source_target_pairs={{8,0},{16,8},{24,16},{0,24},{9,1},{17,9},{25,17},{1,25},{10,2},{18... | collective-permute-start | bytes 294920 | tf_op jit(solution)/shard_map/ppermute | solution.py:19
  10.2 3.4 %copy-start.4 = (f32[256]{0:T(256)S(1)}, f32[256]{0:T(256)}, u32[]{:S(2)}) copy-start(f32[256]{0:T(256)} %param.12) | copy-start | bytes 3076
  10.2 14.8 %copy-start.2 = (f32[3,4,32,8,256]{4,3,2,1,0:T(8,128)S(1)}, f32[3,4,32,8,256]{4,3,2,1,0:T(8,128)}, u32[]{:S(2)}) copy-start(f32[3,4,32,8,256]{4,3,2,1,0:T(8,128)} %param.11) | copy-start | bytes 9437188
  13.1 9.0 %collective-permute-start.2 = (f32[3,4,34,1,256]{4,3,2,1,0:T(1,128)S(1)}, f32[3,4,34,1,256]{4,3,2,1,0:T(1,128)S(1)}, u32[]{:S(2)}, u32[]{:S(2)}) collective-permute-start(f32[3,4,34,1,256]{4,3,2,1,0:T(1,128)S(1)} %get-tuple-element.75), channel_id=1, source_target_pairs={{2,0},{4,2},{6,4},{0,6},{3,1},{5,3},{7,5},{1,7},{10,8},{12,10},{14... | collective-permute-start | bytes 1253384 | tf_op jit(solution)/shard_map/ppermute | solution.py:19
  13.1 11.9 %collective-permute-start.3 = (f32[3,4,34,1,256]{4,3,2,1,0:T(1,128)S(1)}, f32[3,4,34,1,256]{4,3,2,1,0:T(1,128)S(1)}, u32[]{:S(2)}, u32[]{:S(2)}) collective-permute-start(f32[3,4,34,1,256]{4,3,2,1,0:T(1,128)S(1)} %get-tuple-element.76), channel_id=1, source_target_pairs={{0,2},{2,4},{4,6},{6,0},{1,3},{3,5},{5,7},{7,1},{8,10},{10,12},{12... | collective-permute-start | bytes 1253384 | tf_op jit(solution)/shard_map/ppermute | solution.py:17
  30.5 6.6 %collective-permute-start.4 = (f32[3,4,1,8,256]{4,3,2,1,0:T(8,128)S(1)}, f32[3,4,1,8,256]{4,3,2,1,0:T(8,128)S(1)}, u32[]{:S(2)}, u32[]{:S(2)}) collective-permute-start(f32[3,4,1,8,256]{4,3,2,1,0:T(8,128)S(1)} %get-tuple-element.84), channel_id=1, source_target_pairs={{8,0},{16,8},{24,16},{0,24},{9,1},{17,9},{25,17},{1,25},{10,2},{18... | collective-permute-start | bytes 294920 | tf_op jit(solution)/shard_map/ppermute | solution.py:19
  33.9 6.4 %collective-permute-start.5 = (f32[3,4,1,8,256]{4,3,2,1,0:T(8,128)S(1)}, f32[3,4,1,8,256]{4,3,2,1,0:T(8,128)S(1)}, u32[]{:S(2)}, u32[]{:S(2)}) collective-permute-start(f32[3,4,1,8,256]{4,3,2,1,0:T(8,128)S(1)} %get-tuple-element.83), channel_id=1, source_target_pairs={{0,8},{8,16},{16,24},{24,0},{1,9},{9,17},{17,25},{25,1},{2,10},{10... | collective-permute-start | bytes 294920 | tf_op jit(solution)/shard_map/ppermute | solution.py:17
  40.8 9.9 %collective-permute-start.6 = (f32[3,4,34,1,256]{4,3,2,1,0:T(1,128)S(1)}, f32[3,4,34,1,256]{4,3,2,1,0:T(1,128)S(1)}, u32[]{:S(2)}, u32[]{:S(2)}) collective-permute-start(f32[3,4,34,1,256]{4,3,2,1,0:T(1,128)S(1)} %get-tuple-element.73), channel_id=1, source_target_pairs={{2,0},{4,2},{6,4},{0,6},{3,1},{5,3},{7,5},{1,7},{10,8},{12,10},{14... | collective-permute-start | bytes 1253384 | tf_op jit(solution)/shard_map/ppermute | solution.py:19
  40.8 11.0 %collective-permute-start.7 = (f32[3,4,34,1,256]{4,3,2,1,0:T(1,128)S(1)}, f32[3,4,34,1,256]{4,3,2,1,0:T(1,128)S(1)}, u32[]{:S(2)}, u32[]{:S(2)}) collective-permute-start(f32[3,4,34,1,256]{4,3,2,1,0:T(1,128)S(1)} %get-tuple-element.74), channel_id=1, source_target_pairs={{0,2},{2,4},{4,6},{6,0},{1,3},{3,5},{5,7},{7,1},{8,10},{10,12},{12... | collective-permute-start | bytes 1253384 | tf_op jit(solution)/shard_map/ppermute | solution.py:17
  60.3 5.7 %collective-permute-start.8 = (f32[3,4,1,8,256]{4,3,2,1,0:T(8,128)S(1)}, f32[3,4,1,8,256]{4,3,2,1,0:T(8,128)S(1)}, u32[]{:S(2)}, u32[]{:S(2)}) collective-permute-start(f32[3,4,1,8,256]{4,3,2,1,0:T(8,128)S(1)} %get-tuple-element.82), channel_id=1, source_target_pairs={{8,0},{16,8},{24,16},{0,24},{9,1},{17,9},{25,17},{1,25},{10,2},{18... | collective-permute-start | bytes 294920 | tf_op jit(solution)/shard_map/ppermute | solution.py:19
  61.0 6.4 %collective-permute-start.9 = (f32[3,4,1,8,256]{4,3,2,1,0:T(8,128)S(1)}, f32[3,4,1,8,256]{4,3,2,1,0:T(8,128)S(1)}, u32[]{:S(2)}, u32[]{:S(2)}) collective-permute-start(f32[3,4,1,8,256]{4,3,2,1,0:T(8,128)S(1)} %get-tuple-element.81), channel_id=1, source_target_pairs={{0,8},{8,16},{16,24},{24,0},{1,9},{9,17},{17,25},{25,1},{2,10},{10... | collective-permute-start | bytes 294920 | tf_op jit(solution)/shard_map/ppermute | solution.py:17
  67.9 9.0 %collective-permute-start.10 = (f32[3,4,34,1,256]{4,3,2,1,0:T(1,128)S(1)}, f32[3,4,34,1,256]{4,3,2,1,0:T(1,128)S(1)}, u32[]{:S(2)}, u32[]{:S(2)}) collective-permute-start(f32[3,4,34,1,256]{4,3,2,1,0:T(1,128)S(1)} %get-tuple-element.71), channel_id=1, source_target_pairs={{2,0},{4,2},{6,4},{0,6},{3,1},{5,3},{7,5},{1,7},{10,8},{12,10},{14... | collective-permute-start | bytes 1253384 | tf_op jit(solution)/shard_map/ppermute | solution.py:19
  68.0 11.9 %collective-permute-start.11 = (f32[3,4,34,1,256]{4,3,2,1,0:T(1,128)S(1)}, f32[3,4,34,1,256]{4,3,2,1,0:T(1,128)S(1)}, u32[]{:S(2)}, u32[]{:S(2)}) collective-permute-start(f32[3,4,34,1,256]{4,3,2,1,0:T(1,128)S(1)} %get-tuple-element.72), channel_id=1, source_target_pairs={{0,2},{2,4},{4,6},{6,0},{1,3},{3,5},{5,7},{7,1},{8,10},{10,12},{12... | collective-permute-start | bytes 1253384 | tf_op jit(solution)/shard_map/ppermute | solution.py:17
  85.6 4.9 %collective-permute-start.12 = (f32[3,4,1,8,256]{4,3,2,1,0:T(8,128)S(1)}, f32[3,4,1,8,256]{4,3,2,1,0:T(8,128)S(1)}, u32[]{:S(2)}, u32[]{:S(2)}) collective-permute-start(f32[3,4,1,8,256]{4,3,2,1,0:T(8,128)S(1)} %get-tuple-element.80), channel_id=1, source_target_pairs={{8,0},{16,8},{24,16},{0,24},{9,1},{17,9},{25,17},{1,25},{10,2},{18... | collective-permute-start | bytes 294920 | tf_op jit(solution)/shard_map/ppermute | solution.py:19
  86.5 6.6 %collective-permute-start.13 = (f32[3,4,1,8,256]{4,3,2,1,0:T(8,128)S(1)}, f32[3,4,1,8,256]{4,3,2,1,0:T(8,128)S(1)}, u32[]{:S(2)}, u32[]{:S(2)}) collective-permute-start(f32[3,4,1,8,256]{4,3,2,1,0:T(8,128)S(1)} %get-tuple-element.79), channel_id=1, source_target_pairs={{0,8},{8,16},{16,24},{24,0},{1,9},{9,17},{17,25},{25,1},{2,10},{10... | collective-permute-start | bytes 294920 | tf_op jit(solution)/shard_map/ppermute | solution.py:17
  93.6 9.7 %collective-permute-start.14 = (f32[3,4,34,1,256]{4,3,2,1,0:T(1,128)S(1)}, f32[3,4,34,1,256]{4,3,2,1,0:T(1,128)S(1)}, u32[]{:S(2)}, u32[]{:S(2)}) collective-permute-start(f32[3,4,34,1,256]{4,3,2,1,0:T(1,128)S(1)} %get-tuple-element.69), channel_id=1, source_target_pairs={{2,0},{4,2},{6,4},{0,6},{3,1},{5,3},{7,5},{1,7},{10,8},{12,10},{14... | collective-permute-start | bytes 1253384 | tf_op jit(solution)/shard_map/ppermute | solution.py:19
  94.0 11.7 %collective-permute-start.15 = (f32[3,4,34,1,256]{4,3,2,1,0:T(1,128)S(1)}, f32[3,4,34,1,256]{4,3,2,1,0:T(1,128)S(1)}, u32[]{:S(2)}, u32[]{:S(2)}) collective-permute-start(f32[3,4,34,1,256]{4,3,2,1,0:T(1,128)S(1)} %get-tuple-element.70), channel_id=1, source_target_pairs={{0,2},{2,4},{4,6},{6,0},{1,3},{3,5},{5,7},{7,1},{8,10},{10,12},{12... | collective-permute-start | bytes 1253384 | tf_op jit(solution)/shard_map/ppermute | solution.py:17
  109.4 70.1 %collective-permute-start.16 = (f32[3,4,32,8,256]{4,3,2,1,0:T(8,128)S(1)}, f32[3,4,32,8,256]{4,3,2,1,0:T(8,128)}, u32[]{:S(2)}, u32[]{:S(2)}) collective-permute-start(f32[3,4,32,8,256]{4,3,2,1,0:T(8,128)S(1)} %get-tuple-element.78), channel_id=1, source_target_pairs={{0,1},{1,0},{2,3},{3,2},{4,5},{5,4},{6,7},{7,6},{8,9},{9,8},{10,11... | collective-permute-start | bytes 9437192 | tf_op jit(solution)/shard_map/ppermute | solution.py:113
  184.1 4.5 %copy-start.3 = (f32[3,16,32,8,256]{4,3,2,1,0:T(8,128)}, f32[3,16,32,8,256]{4,3,2,1,0:T(8,128)S(1)}, u32[]{:S(2)}) copy-start(f32[3,16,32,8,256]{4,3,2,1,0:T(8,128)S(1)} %pad_maximum_fusion) | copy-start | bytes 37748740
  315.5 13.5 %copy-start.1 = (f32[256,256]{1,0:T(8,128)S(1)}, f32[256,256]{1,0:T(8,128)}, u32[]{:S(2)}) copy-start(f32[256,256]{1,0:T(8,128)} %param.13) | copy-start | bytes 786436
